TPU v7x, 32 devices: a whole 2x2x4 slice. The times are simulated.
32 devices in a mesh: group: 2 (over y), seq: 4 (over z), exp: 2 (over x), tp: 2 (over core).
Axes of the slice: x: 2, y: 2, z: 4, core: 2. Of those that a mesh axis runs over, the one named last changes fastest.
Arguments:
- queries: bfloat16 [4, 512, 4096], P(('group', 'exp'), ('seq', 'tp')), parts along dimension 0, may hold values from -18 to 18
- keys_values: bfloat16 [4, 768, 2, 1024], P(('group', 'exp'), ('seq', 'tp')), parts along dimension 0, may hold values from -18 to 18
- prompt_lengths: int32 [4], P(('group', 'exp')), parts along dimension 0, may hold values from 1 to 256, 384 in all
- routes: int32 [4, 512, 8], P(('group', 'exp'), ('seq', 'tp')), parts along dimension 0, may hold values from 0 to 63, all different within a row; in each aligned block of 64 rows (0 to 63, 64 to 127, ..., all dimensions but the last counted through in order) at most 16 rows name the same one
- gate_weights: float32 [4, 512, 8], P(('group', 'exp'), ('seq', 'tp')), parts along dimension 0, may hold values from 0.05 to 0.5
- norm_gain: float32 [4096], replicated, may hold values from 0.5 to 1.5
- w_gate: bfloat16 [2, 4096, 2048], P('tp', None, 'seq'), may hold values from -0.09375 to 0.09375
- w_up: bfloat16 [2, 4096, 2048], P('tp', None, 'seq'), may hold values from -0.09375 to 0.09375
- w_down: bfloat16 [2, 2048, 4096], P('tp', 'seq'), may hold values from -0.125 to 0.125
Outputs:
- mixed: bfloat16 [4, 512, 4096], P(('group', 'exp'), ('seq', 'tp')), parts along dimension 0
There are 2 independent parts, one for each index of `group`. A program takes and returns all parts, laid end to end along the dimension named above; an argument that names none is the same for every part. Nothing has to cross between parts.
Inputs may be any that keep to these rules, and one draw needn't show every extreme that they name: Each token's 8 routes name different experts. Among the 64 consecutive tokens of one device no expert is named by more than 16 tokens, a bound that some block reaches.
All inputs are finite; a program needn't handle non-finite values. No bound on the sum of `prompt_lengths` on one device may be relied on, other than what follows from the above.
Results may differ from a plain program's by a relative error of at most 0.02.
Values may be sent and summed in bfloat16 or wider, within the bound.
A program may use at most 128 MiB of HBM per device.

v0:
```python
import functools
import math

import jax
import jax.numpy as jnp
from jax import lax
from jax.experimental import pallas as pl
from jax.experimental.pallas import tpu as pltpu
from jax.sharding import PartitionSpec as P

HEADS = 32
KV_HEADS = 8
HEAD_DIM = 128
PROMPT = 256
CAP = 16
LEAD = 8
SUM_CHUNKS = 4
ROW_CHUNKS = 2

epsilon = 1e-06
masked_score = -1e30
MESH = pl.DeviceIdType.MESH
F32 = jnp.float32
BF16 = jnp.bfloat16


def kernel(
    n, plen_ref, kv_ref, routes_ref, gates_ref, gain_ref, q_hbm, wg_hbm, wu_hbm, wd_hbm,
    out_ref,
    q_ref, wg, wu, wd, kvbuf, att, xsel, xbuf, part, rbuf, fin, ret, acc,
    w_sem, kv_local, kv_send, kv_recv, x_send, x_recv, xs_send, r_send, r_recv, y_send, y_recv,
):
    z = lax.axis_index("seq")
    c = lax.axis_index("tp")
    sib = 1 - c
    has_left = z > 0
    has_right = z < n - 1
    left, right, other = {"seq": z - 1}, {"seq": z + 1}, {"tp": sib}
    tokens = q_ref.shape[0]
    piece = kv_ref.shape[0]
    groups = HEADS // KV_HEADS
    span = groups * HEAD_DIM
    width = att.shape[1]
    two = 2

    loads = [
        pltpu.make_async_copy(q_hbm, q_ref, w_sem.at[0]),
        pltpu.make_async_copy(wg_hbm, wg, w_sem.at[1]),
        pltpu.make_async_copy(wu_hbm, wu, w_sem.at[2]),
        pltpu.make_async_copy(wd_hbm, wd, w_sem.at[3]),
    ]
    own_kv = [
        pltpu.make_async_copy(
            kv_ref.at[:, pl.ds((s * KV_HEADS + h) * HEAD_DIM, HEAD_DIM)],
            kvbuf.at[h, s, z, c], kv_local.at[h, s],
        )
        for h in range(KV_HEADS) for s in range(2)
    ]
    for copy in own_kv:
        copy.start()
    loads[0].start()

    barrier = pltpu.get_barrier_semaphore()

    @pl.when(has_left)
    def _():
        pl.semaphore_signal(barrier, inc=1, device_id=left, device_id_type=MESH)

    @pl.when(has_right)
    def _():
        pl.semaphore_signal(barrier, inc=1, device_id=right, device_id_type=MESH)

    pl.semaphore_signal(barrier, inc=1, device_id=other, device_id_type=MESH)

    for copy in own_kv:
        copy.wait()
    pl.semaphore_wait(barrier, 1 + has_left.astype(jnp.int32) + has_right.astype(jnp.int32))

    def remote(src, dst, send, recv, device):
        return pltpu.make_async_remote_copy(
            src_ref=src, dst_ref=dst, send_sem=send, recv_sem=recv,
            device_id=device, device_id_type=MESH,
        )

    def kv_copy(h, oz, oc, way, device):
        slot = kvbuf.at[h, :, oz, oc]
        return remote(slot, slot, kv_send.at[h, oz, way], kv_recv.at[h, oz, oc], device)

    def send_own(h):
        @pl.when(has_left)
        def _():
            kv_copy(h, z, c, 0, left).start()

        @pl.when(has_right)
        def _():
            kv_copy(h, z, c, 1, right).start()

        kv_copy(h, z, c, 2, other).start()

    for h in range(LEAD):
        send_own(h)
    for load in loads[1:]:
        load.start()
    loads[0].wait()

    plen = plen_ref[0]
    keys = n * two * piece
    position = lax.broadcasted_iota(jnp.int32, (1, keys), 1)
    allowed = (position >= PROMPT) | (position < plen)

    def attend(h):
        base = pl.multiple_of(h * span, span)
        query = jnp.concatenate(
            [q_ref[:, pl.ds(base + g * HEAD_DIM, HEAD_DIM)] for g in range(groups)], axis=0
        )
        key_rows = kvbuf[h, 0].reshape(keys, HEAD_DIM)
        value_rows = kvbuf[h, 1].reshape(keys, HEAD_DIM)
        scores = lax.dot_general(
            query, key_rows, (((1,), (1,)), ((), ())), preferred_element_type=F32
        ) * (1.0 / math.sqrt(HEAD_DIM))
        scores = jnp.where(allowed, scores, masked_score)
        weights = jnp.exp(scores - jnp.max(scores, axis=1, keepdims=True))
        total = jnp.sum(weights, axis=1, keepdims=True)
        summed = jnp.dot(weights.astype(BF16), value_rows, preferred_element_type=F32)
        result = (summed / total).astype(BF16)
        for g in range(groups):
            att[:, pl.ds(base + g * HEAD_DIM, HEAD_DIM)] = result[g * tokens:(g + 1) * tokens]

    def kv_round(r, carry):
        @pl.when(r + LEAD < KV_HEADS)
        def _():
            send_own(r + LEAD)

        for d in range(1, n):
            h = r - (d - 1)
            live = (h >= 0) & (h < KV_HEADS)

            @pl.when(live & (z - d >= 0))
            def _():
                kv_copy(h, z - d, c, 2, other).wait_recv()

                @pl.when(has_right)
                def _():
                    kv_copy(h, z - d, c, 1, right).start()

                kv_copy(h, z - d, c, 2, other).start()

            @pl.when(live & (z + d < n))
            def _():
                kv_copy(h, z + d, c, 2, other).wait_recv()

                @pl.when(has_left)
                def _():
                    kv_copy(h, z + d, c, 0, left).start()

                kv_copy(h, z + d, c, 2, other).start()

        done = r - (n - 1)

        @pl.when(done >= 0)
        def _():
            for oz in range(n):
                kv_copy(done, oz, sib, 2, other).wait_recv()
            attend(done)

        return carry

    lax.fori_loop(0, KV_HEADS + n - 1, kv_round, 0)

    attended = att[...].astype(F32)
    mean_square = jnp.mean(attended * attended, axis=1, keepdims=True)
    normed = (attended * lax.rsqrt(mean_square + epsilon) * gain_ref[...]).astype(BF16)
    routes = routes_ref[...]
    gates = gates_ref[...]
    tri = (
        lax.broadcasted_iota(jnp.int32, (tokens, tokens), 0)
        <= lax.broadcasted_iota(jnp.int32, (tokens, tokens), 1)
    ).astype(F32)
    slots = lax.broadcasted_iota(jnp.int32, (CAP, tokens), 0).astype(F32)
    combine = []
    for e in range(two):
        same = routes == e
        hit = jnp.max(same.astype(F32), axis=0, keepdims=True)
        gate = jnp.sum(jnp.where(same, gates, 0.0), axis=0, keepdims=True)
        rank = jnp.dot(jnp.broadcast_to(hit, (CAP, tokens)), tri, preferred_element_type=F32)
        select = jnp.where((rank - 1.0 == slots) & (hit > 0.0), 1.0, 0.0)
        combine.append(select * gate)
        xsel[e] = jnp.dot(select.astype(BF16), normed, preferred_element_type=F32).astype(BF16)
    xbuf[z, c] = xsel[c]

    cut = width // ROW_CHUNKS

    def row_copy(oz, oc, k, way, device):
        slot = xbuf.at[oz, oc, :, pl.ds(k * cut, cut)]
        return remote(slot, slot, x_send.at[oz, oc, k, way], x_recv.at[oz, oc, k], device)

    def sib_copy(oc, k):
        cols = pl.ds(k * cut, cut)
        return remote(
            xsel.at[sib, :, cols], xbuf.at[z, oc, :, cols], xs_send.at[k], x_recv.at[z, oc, k], other
        )

    for k in range(ROW_CHUNKS):
        sib_copy(c, k).start()

    def pass_rows(oz, oc, k, go_left, go_right):
        if go_left is not False:
            @pl.when(go_left)
            def _():
                row_copy(oz, oc, k, 0, left).start()

        if go_right is not False:
            @pl.when(go_right)
            def _():
                row_copy(oz, oc, k, 1, right).start()

    for k in range(ROW_CHUNKS):
        pass_rows(z, c, k, has_left, has_right)
    for k in range(ROW_CHUNKS):
        sib_copy(sib, k).wait_recv()
        pass_rows(z, sib, k, has_left, has_right)
    for load in loads[1:]:
        load.wait()

    rows_here = two * CAP
    strip = width // SUM_CHUNKS

    def expert(origin):
        rows = xbuf[origin].reshape(rows_here, width)
        gate_part = jnp.dot(rows, wg[...], preferred_element_type=F32)
        up_part = jnp.dot(rows, wu[...], preferred_element_type=F32)
        hidden = (gate_part / (1.0 + jnp.exp(-gate_part)) * up_part).astype(BF16)
        for k in range(SUM_CHUNKS):
            part[origin, k] = jnp.dot(
                hidden, wd[:, k * strip:(k + 1) * strip], preferred_element_type=F32
            ).astype(BF16)

    def sum_copy(way, dest, k, device):
        return remote(
            part.at[dest, k], rbuf.at[way, dest, k], r_send.at[way, dest, k], r_recv.at[way, dest, k],
            device,
        )

    def pass_sum(way, dest, joins, device):
        for k in range(SUM_CHUNKS):
            @pl.when(joins)
            def _():
                sum_copy(way, dest, k, device).wait_recv()
                part[dest, k] = (part[dest, k].astype(F32) + rbuf[way, dest, k].astype(F32)).astype(BF16)

            sum_copy(way, dest, k, device).start()

    def expert_round(t, carry):
        for oc in range(two):
            for k in range(ROW_CHUNKS):
                slot = jnp.where(oc == 0, c, sib)

                @pl.when((t > 0) & (z - t >= 0))
                def _():
                    row_copy(z - t, slot, k, 1, right).wait_recv()
                    pass_rows(z - t, slot, k, False, has_right)

                @pl.when((t > 0) & (z + t < n))
                def _():
                    row_copy(z + t, slot, k, 0, left).wait_recv()
                    pass_rows(z + t, slot, k, has_left, False)

        def side(k, inner):
            origin = jnp.where(k == 0, z - t, z + t)

            @pl.when((origin >= 0) & (origin < n) & ((k == 0) | (t > 0)))
            def _():
                expert(origin)

            return inner

        lax.fori_loop(0, 2, side, 0)

        dest = t - z

        @pl.when((dest > z) & (dest < n))
        def _():
            pass_sum(0, dest, has_left, right)

        mirror = n - 1 - z
        back = t - mirror
        home = n - 1 - back

        @pl.when((back > mirror) & (back < n))
        def _():
            pass_sum(1, home, has_right, left)

        return carry

    lax.fori_loop(0, 2 * n - 2, expert_round, 0)

    def result_copy(oc, k):
        cols = pl.ds(k * strip, strip)
        return remote(fin.at[sib, :, cols], ret.at[oc, :, cols], y_send.at[k], y_recv.at[k], other)

    for k in range(SUM_CHUNKS):
        cols = slice(k * strip, (k + 1) * strip)
        acc[...] = part[z, k].astype(F32)

        @pl.when(has_left)
        def _():
            sum_copy(0, z, k, right).wait_recv()
            acc[...] += rbuf[0, z, k].astype(F32)

        @pl.when(has_right)
        def _():
            sum_copy(1, z, k, left).wait_recv()
            acc[...] += rbuf[1, z, k].astype(F32)

        fin[:, :, cols] = acc[...].astype(BF16).reshape(two, CAP, strip)
        result_copy(c, k).start()
        ret[c, :, cols] = fin[c, :, cols]

    cw = jnp.transpose(jnp.concatenate(combine, axis=0))
    first = cw.astype(BF16)
    rest = cw - first.astype(F32)
    second = rest.astype(BF16)
    third = (rest - second.astype(F32)).astype(BF16)
    for k in range(SUM_CHUNKS):
        cols = slice(k * strip, (k + 1) * strip)
        result_copy(sib, k).wait_recv()
        returned = ret[:, :, cols].reshape(rows_here, strip)
        total = (
            jnp.dot(first, returned, preferred_element_type=F32)
            + jnp.dot(second, returned, preferred_element_type=F32)
            + jnp.dot(third, returned, preferred_element_type=F32)
        )
        out_ref[:, cols] = (att[:, cols].astype(F32) + total).astype(BF16)

    for k in range(SUM_CHUNKS):
        result_copy(c, k).wait_send()
    for k in range(ROW_CHUNKS):
        sib_copy(c, k).wait_send()

    def drain_kv(h, carry):
        for oz in range(n):
            @pl.when(has_left & (oz >= z))
            def _():
                kv_copy(h, oz, c, 0, left).wait_send()

            @pl.when(has_right & (oz <= z))
            def _():
                kv_copy(h, oz, c, 1, right).wait_send()

            kv_copy(h, oz, c, 2, other).wait_send()
        return carry

    lax.fori_loop(0, KV_HEADS, drain_kv, 0)
    for oz in range(n):
        for oc in range(two):
            for k in range(ROW_CHUNKS):
                @pl.when(has_left & (oz >= z))
                def _():
                    row_copy(oz, oc, k, 0, left).wait_send()

                @pl.when(has_right & (oz <= z))
                def _():
                    row_copy(oz, oc, k, 1, right).wait_send()

        for k in range(SUM_CHUNKS):
            @pl.when(oz > z)
            def _():
                sum_copy(0, oz, k, right).wait_send()

            @pl.when(oz < z)
            def _():
                sum_copy(1, oz, k, left).wait_send()


def body(
    queries, keys_values, prompt_lengths, routes, gate_weights, norm_gain, w_gate, w_up, w_down
):
    n = lax.axis_size("seq")
    tokens, width = queries.shape[1:]
    piece = keys_values.shape[1]
    ff = w_gate.shape[2]
    kv = keys_values[0].reshape(piece, 2 * KV_HEADS * HEAD_DIM)
    strip = width // SUM_CHUNKS
    vmem = pl.BlockSpec(memory_space=pltpu.VMEM)
    hbm = pl.BlockSpec(memory_space=pltpu.HBM)
    dma = pltpu.SemaphoreType.DMA
    mixed = pl.pallas_call(
        functools.partial(kernel, n),
        out_shape=jax.ShapeDtypeStruct((tokens, width), BF16),
        in_specs=[pl.BlockSpec(memory_space=pltpu.SMEM), vmem, vmem, vmem, vmem, hbm, hbm, hbm, hbm],
        out_specs=vmem,
        scratch_shapes=[
            pltpu.VMEM((tokens, width), BF16),
            pltpu.VMEM((width, ff), BF16),
            pltpu.VMEM((width, ff), BF16),
            pltpu.VMEM((ff, width), BF16),
            pltpu.VMEM((KV_HEADS, 2, n, 2, piece, HEAD_DIM), BF16),
            pltpu.VMEM((tokens, width), BF16),
            pltpu.VMEM((2, CAP, width), BF16),
            pltpu.VMEM((n, 2, CAP, width), BF16),
            pltpu.VMEM((n, SUM_CHUNKS, 2 * CAP, strip), BF16),
            pltpu.VMEM((2, n, SUM_CHUNKS, 2 * CAP, strip), BF16),
            pltpu.VMEM((2, CAP, width), BF16),
            pltpu.VMEM((2, CAP, width), BF16),
            pltpu.VMEM((2 * CAP, strip), F32),
            dma((4,)),
            dma((KV_HEADS, 2)),
            dma((KV_HEADS, n, 3)),
            dma((KV_HEADS, n, 2)),
            dma((n, 2, ROW_CHUNKS, 2)),
            dma((n, 2, ROW_CHUNKS)),
            dma((ROW_CHUNKS,)),
            dma((2, n, SUM_CHUNKS)),
            dma((2, n, SUM_CHUNKS)),
            dma((SUM_CHUNKS,)),
            dma((SUM_CHUNKS,)),
        ],
        compiler_params=pltpu.CompilerParams(
            collective_id=0, has_side_effects=True, vmem_limit_bytes=56 * 1024 * 1024
        ),
    )(
        prompt_lengths, kv, routes[0].T, gate_weights[0].T, norm_gain[None], queries[0],
        w_gate[0], w_up[0], w_down[0],
    )
    return mixed[None]


def solution(mesh):
    return jax.shard_map(
        body,
        mesh=mesh,
        in_specs=(
            P(("group", "exp"), ("seq", "tp"), None),
            P(("group", "exp"), ("seq", "tp"), None, None),
            P(("group", "exp")),
            P(("group", "exp"), ("seq", "tp"), None),
            P(("group", "exp"), ("seq", "tp"), None),
            P(),
            P("tp", None, "seq"),
            P("tp", None, "seq"),
            P("tp", "seq", None),
        ),
        out_specs=P(("group", "exp"), ("seq", "tp"), None),
        check_vma=False,
    )
```

profile of v0, /device:TPU:0, one launch (start us, length us, event | category | flops | bytes accessed | tf_op | source)
XLA Modules:
  0.0 79.1 jit_solution(6606412665804105650)
XLA Ops:
  0.7 1.8 %copy.10 = bf16[12,8,2,1024]{3,1,2,0:T(8,128)(2,1)} copy(bf16[12,8,2,1024]{3,2,1,0:T(2,128)(2,1)} %bitcast.21) | data formatting | bytes 786432
  2.5 74.8 %shard_map.91 = bf16[64,4096]{1,0:T(8,128)(2,1)} custom-call(s32[1]{0:T(128)S(6)} %copy.12.plen_ref, bf16[96,2048]{1,0:T(8,128)(2,1)} %bitcast.19, s32[8,64]{1,0:T(8,128)} %bitcast.23, f32[8,64]{1,0:T(8,128)} %bitcast.24, f32[1,4096]{1,0:T(1,128)} %bitcast.22, bf16[64,4096]{1,0:T(8,128)(2,1)} %bitcast.20, bf16[4096,512]{1,0:T(8,128)(2,1)} %bitcast.15, ...), custom_call_target="tpu_custom_call" | custom-call | tf_op jit(solution)/shard_map/pallas_call | solution.py:387
  77.2 1.9 %copy.13 = bf16[1,64,4096]{2,1,0:T(8,128)(2,1)} copy(bf16[1,64,4096]{2,1,0:T(8,128)(2,1)} %bitcast.18) | data formatting | bytes 1048576
where the time goes:
time: 79.3 us; the launch traced here: 79.1 us
  Pallas kernels  74.8 us (94%)
  local copies, waits for them, and re-layouts  3.69 us (5%)
    pallas_call x1, Pallas kernels, body(): pl.pallas_call(functools.partial(kernel, n), out_shape=jax.ShapeDtypeStru...  74.8 us
    unnamed x2, local copies, waits for them, and re-layouts  3.69 us

commit v1 on v0

v1 whole, which is shorter than its diff:
```python
import functools
import math

import jax
import jax.numpy as jnp
from jax import lax
from jax.experimental import pallas as pl
from jax.experimental.pallas import tpu as pltpu
from jax.sharding import PartitionSpec as P

HEADS = 32
KV_HEADS = 8
HEAD_DIM = 128
PROMPT = 256
CAP = 16
LEAD = 4
SHIP = 5

epsilon = 1e-06
masked_score = -1e30
MESH = pl.DeviceIdType.MESH
F32 = jnp.float32
BF16 = jnp.bfloat16


def kernel(
    n, plen_ref, routes_hbm, gates_hbm, gain_hbm, kv_hbm, q_hbm, wg_hbm, wu_hbm, wd_hbm,
    out_ref,
    routes_ref, gates_ref, gain_ref, raw, q_ref, qx, ox, wg, wu, wd, kvbuf, att, sel, xsel, xbuf, part, rbuf, fin, ret,
    small_sem, w_sem, raw_sem, q_sem, kv_send, kv_recv, q_send, q_recv, o_send, o_recv,
    xs_send, xs_recv, x_send, x_recv, r_send, r_recv, y_send, y_recv,
):
    z = lax.axis_index("seq")
    c = lax.axis_index("tp")
    sib = 1 - c
    has_left = z > 0
    has_right = z < n - 1
    left, right, other = {"seq": z - 1}, {"seq": z + 1}, {"tp": sib}
    tokens = q_ref.shape[1]
    piece = raw.shape[1]
    groups = HEADS // KV_HEADS
    span = groups * HEAD_DIM
    width = KV_HEADS * span
    ff = wg.shape[1]
    two = 2
    keys = n * two * piece
    rows_here = two * CAP
    ship = SHIP if n >= 4 else 0

    is_end = (z == 0) | (z == n - 1)
    helps = (z == 1) | (z == n - 2)
    end = {"seq": jnp.where(z == 1, 0, n - 1)}
    helper = {"seq": jnp.where(z == 0, 1, n - 2)}

    barrier = pltpu.get_barrier_semaphore()

    @pl.when(has_left)
    def _():
        pl.semaphore_signal(barrier, inc=1, device_id=left, device_id_type=MESH)

    @pl.when(has_right)
    def _():
        pl.semaphore_signal(barrier, inc=1, device_id=right, device_id_type=MESH)

    pl.semaphore_signal(barrier, inc=1, device_id=other, device_id_type=MESH)

    own_kv = [
        pltpu.make_async_copy(
            kv_hbm.at[:, :, pl.ds(h * HEAD_DIM, HEAD_DIM)], raw.at[h], raw_sem.at[h]
        )
        for h in range(KV_HEADS)
    ]
    own_q = [
        pltpu.make_async_copy(q_hbm.at[:, pl.ds(h * span, span)], q_ref.at[h], q_sem.at[h])
        for h in range(KV_HEADS)
    ]
    small = [
        pltpu.make_async_copy(routes_hbm, routes_ref, small_sem.at[0]),
        pltpu.make_async_copy(gates_hbm, gates_ref, small_sem.at[1]),
        pltpu.make_async_copy(gain_hbm, gain_ref, small_sem.at[2]),
    ]
    loads = [
        pltpu.make_async_copy(wg_hbm, wg, w_sem.at[0]),
        pltpu.make_async_copy(wu_hbm, wu, w_sem.at[1]),
        pltpu.make_async_copy(wd_hbm, wd, w_sem.at[2]),
    ]
    for copy in own_kv + own_q + small:
        copy.start()

    row = lax.broadcasted_iota(jnp.int32, (two * piece, two * piece), 0)
    col = lax.broadcasted_iota(jnp.int32, (two * piece, two * piece), 1)
    source = jnp.where(row < piece, 2 * row, 2 * (row - piece) + 1)
    unzip = (col == source).astype(BF16)
    def remote(src, dst, send, recv, device):
        return pltpu.make_async_remote_copy(
            src_ref=src, dst_ref=dst, send_sem=send, recv_sem=recv,
            device_id=device, device_id_type=MESH,
        )

    def kv_copy(h, oz, oc, way, device):
        slot = kvbuf.at[h, :, oz, oc]
        return remote(slot, slot, kv_send.at[h, oz, way], kv_recv.at[h, oz, oc], device)

    def gathers(h):
        return jnp.logical_not(is_end & (h < ship))

    def goes_left(h):
        return has_left & jnp.logical_not((z == 1) & (h < ship))

    def goes_right(h):
        return has_right & jnp.logical_not((z == n - 2) & (h < ship))

    def query_copy(h):
        return remote(q_ref.at[h], qx.at[h], q_send.at[h], q_recv.at[h], helper)

    def answer_copy(h):
        return remote(ox.at[h], att.at[h], o_send.at[h], o_recv.at[h], end)

    def send_own(h):
        @pl.when(goes_left(h))
        def _():
            kv_copy(h, z, c, 0, left).start()

        @pl.when(goes_right(h))
        def _():
            kv_copy(h, z, c, 1, right).start()

        @pl.when(gathers(h))
        def _():
            kv_copy(h, z, c, 2, other).start()

        if ship:
            @pl.when(is_end & (h < ship))
            def _():
                query_copy(h).start()

    pl.semaphore_wait(barrier, 1 + has_left.astype(jnp.int32) + has_right.astype(jnp.int32))
    for h in range(KV_HEADS):
        own_kv[h].wait()
        own_q[h].wait()
        pairs = raw.at[h].reshape(two * piece, HEAD_DIM)[...]
        parted = jnp.dot(unzip, pairs, preferred_element_type=F32).astype(BF16)
        kvbuf[h, 0, z, c] = parted[:piece]
        kvbuf[h, 1, z, c] = parted[piece:]
        if 1 <= h <= LEAD:
            send_own(h - 1)
    if LEAD == KV_HEADS:
        send_own(LEAD - 1)
    for load in loads:
        load.start()

    for copy in small:
        copy.wait()
    plen = plen_ref[0]
    position = lax.broadcasted_iota(jnp.int32, (1, keys), 1)
    allowed = (position >= PROMPT) | (position < plen)

    routes = routes_ref[...]
    gates = gates_ref[...]
    tri = (
        lax.broadcasted_iota(jnp.int32, (tokens, tokens), 0)
        <= lax.broadcasted_iota(jnp.int32, (tokens, tokens), 1)
    ).astype(F32)
    slots = lax.broadcasted_iota(jnp.int32, (CAP, tokens), 0).astype(F32)
    combine = []
    for e in range(two):
        same = routes == e
        hit = jnp.max(same.astype(F32), axis=0, keepdims=True)
        gate = jnp.sum(jnp.where(same, gates, 0.0), axis=0, keepdims=True)
        rank = jnp.dot(jnp.broadcast_to(hit, (CAP, tokens)), tri, preferred_element_type=F32)
        select = jnp.where((rank - 1.0 == slots) & (hit > 0.0), 1.0, 0.0)
        combine.append(select * gate)
        sel[pl.ds(e * CAP, CAP), :] = select.astype(BF16)

    def attend(h, source, target):
        query = jnp.concatenate(
            [source[h, :, g * HEAD_DIM:(g + 1) * HEAD_DIM] for g in range(groups)], axis=0
        )
        key_rows = kvbuf[h, 0].reshape(keys, HEAD_DIM)
        value_rows = kvbuf[h, 1].reshape(keys, HEAD_DIM)
        scores = lax.dot_general(
            query, key_rows, (((1,), (1,)), ((), ())), preferred_element_type=F32
        ) * (1.0 / math.sqrt(HEAD_DIM))
        scores = jnp.where(allowed, scores, masked_score)
        weights = jnp.exp(scores - jnp.max(scores, axis=1, keepdims=True))
        total = jnp.sum(weights, axis=1, keepdims=True)
        summed = jnp.dot(weights.astype(BF16), value_rows, preferred_element_type=F32)
        result = (summed / total).astype(BF16)
        for g in range(groups):
            target[h, :, g * HEAD_DIM:(g + 1) * HEAD_DIM] = result[g * tokens:(g + 1) * tokens]

    def row_copy(oz, h, way, device):
        slot = xbuf.at[oz, h]
        return remote(slot, slot, x_send.at[oz, h, way], x_recv.at[oz, h], device)

    def sib_copy(h):
        return remote(xsel.at[h, sib], xbuf.at[z, h, c], xs_send.at[h], xs_recv.at[h], other)

    reach = jnp.maximum(z, n - 1 - z)

    def kv_round(r, carry):
        @pl.when(r + LEAD < KV_HEADS)
        def _():
            send_own(r + LEAD)

        for d in range(1, n):
            h = r - (d - 1)
            live = (h >= 0) & (h < KV_HEADS) & gathers(h)

            @pl.when(live & (z - d >= 0))
            def _():
                kv_copy(h, z - d, c, 2, other).wait_recv()

                @pl.when(goes_right(h))
                def _():
                    kv_copy(h, z - d, c, 1, right).start()

                kv_copy(h, z - d, c, 2, other).start()

            @pl.when(live & (z + d < n))
            def _():
                kv_copy(h, z + d, c, 2, other).wait_recv()

                @pl.when(goes_left(h))
                def _():
                    kv_copy(h, z + d, c, 0, left).start()

                kv_copy(h, z + d, c, 2, other).start()

        passed = r - reach - 2

        @pl.when((passed >= 0) & (passed < KV_HEADS))
        def _():
            sib_copy(passed).wait_recv()

            @pl.when(has_left)
            def _():
                row_copy(z, passed, 0, left).start()

            @pl.when(has_right)
            def _():
                row_copy(z, passed, 1, right).start()

        chosen = r - reach - 1

        @pl.when((chosen >= 0) & (chosen < KV_HEADS))
        def _():
            if ship:
                @pl.when(is_end & (chosen < ship))
                def _():
                    answer_copy(chosen).wait_recv()

            picked = jnp.dot(sel[...], att[chosen], preferred_element_type=F32).astype(BF16)
            xsel[chosen] = picked.reshape(two, CAP, span)
            xbuf[z, chosen, c] = xsel[chosen, c]
            sib_copy(chosen).start()

        done = r - reach

        @pl.when((done >= 0) & (done < KV_HEADS) & gathers(done))
        def _():
            for oz in range(n):
                kv_copy(done, oz, sib, 2, other).wait_recv()

            if ship:
                @pl.when(helps & (done < ship))
                def _():
                    query_copy(done).wait_recv()
                    attend(done, qx, ox)
                    answer_copy(done).start()

            attend(done, q_ref, att)

        return carry

    lax.fori_loop(0, KV_HEADS + n + 1, kv_round, 0)

    for load in loads:
        load.wait()

    def sum_copy(way, dest, k, device):
        return remote(
            part.at[dest, k], rbuf.at[way, dest, k], r_send.at[way, dest, k], r_recv.at[way, dest, k],
            device,
        )

    def expert(origins, arrive, leave):
        count = len(origins)
        gate_part = jnp.zeros((count * rows_here, ff), F32)
        up_part = jnp.zeros((count * rows_here, ff), F32)
        squares = jnp.zeros((count * rows_here, 1), F32)
        for h in range(KV_HEADS):
            cols = slice(h * span, (h + 1) * span)
            arrive(h)
            rows = jnp.concatenate(
                [xbuf[origin, h].reshape(rows_here, span) for origin in origins], axis=0
            ).astype(F32)
            squares += jnp.sum(rows * rows, axis=1, keepdims=True)
            scaled = (rows * gain_ref[:, cols]).astype(BF16)
            gate_part += jnp.dot(scaled, wg[cols, :], preferred_element_type=F32)
            up_part += jnp.dot(scaled, wu[cols, :], preferred_element_type=F32)
        inverse = lax.rsqrt(squares * (1.0 / width) + epsilon)
        gate_part *= inverse
        up_part *= inverse
        hidden = (gate_part / (1.0 + jnp.exp(-gate_part)) * up_part).astype(BF16)
        for k in range(KV_HEADS):
            cols = slice(k * span, (k + 1) * span)
            block = jnp.dot(hidden, wd[:, cols], preferred_element_type=F32).astype(BF16)
            for i, origin in enumerate(origins):
                part[origin, k] = block[i * rows_here:(i + 1) * rows_here]
            leave(k)

    def take_from_left(oz, h):
        row_copy(oz, h, 1, right).wait_recv()

        @pl.when(has_right)
        def _():
            row_copy(oz, h, 1, right).start()

    def take_from_right(oz, h):
        row_copy(oz, h, 0, left).wait_recv()

        @pl.when(has_left)
        def _():
            row_copy(oz, h, 0, left).start()

    def start_sum(origin, k):
        @pl.when(z == 0)
        def _():
            sum_copy(0, origin, k, right).start()

        @pl.when(z == n - 1)
        def _():
            sum_copy(1, origin, k, left).start()

    def single(t, with_own):
        from_left = z - t >= 0
        origin = jnp.where(from_left, z - t, z + t)

        def arrive(h):
            @pl.when(from_left)
            def _():
                take_from_left(z - t, h)

            @pl.when(jnp.logical_not(from_left))
            def _():
                take_from_right(z + t, h)

        expert([origin, z] if with_own else [origin], arrive, lambda k: start_sum(origin, k))

    def near(h):
        take_from_left(z - 1, h)
        take_from_right(z + 1, h)

    @pl.when(is_end)
    def _():
        single(1, True)

    @pl.when(jnp.logical_not(is_end))
    def _():
        expert([z - 1, z + 1, z], near, lambda k: None)

    def pass_sum(way, dest, device):
        for k in range(KV_HEADS):
            sum_copy(way, dest, k, device).wait_recv()
            part[dest, k] = (part[dest, k].astype(F32) + rbuf[way, dest, k].astype(F32)).astype(BF16)
            sum_copy(way, dest, k, device).start()

    def expert_round(t, carry):
        def side(k, inner):
            origin = jnp.where(k == 0, z - t, z + t)

            @pl.when((origin >= 0) & (origin < n))
            def _():
                def arrive(h):
                    @pl.when(k == 0)
                    def _():
                        take_from_left(origin, h)

                    @pl.when(k == 1)
                    def _():
                        take_from_right(origin, h)

                expert([origin], arrive, lambda k: start_sum(origin, k))

            return inner

        lax.fori_loop(0, 2, side, 0)

        dest = t - z

        @pl.when(has_left & (dest > z) & (dest < n))
        def _():
            pass_sum(0, dest, right)

        mirror = n - 1 - z
        back = t - mirror
        home = n - 1 - back

        @pl.when(has_right & (back > mirror) & (back < n))
        def _():
            pass_sum(1, home, left)

        return carry

    lax.fori_loop(2, 2 * n - 2, expert_round, 0)

    def result_copy(oc, k):
        return remote(fin.at[k, sib], ret.at[oc, k], y_send.at[k], y_recv.at[k], other)

    for k in range(KV_HEADS):
        @pl.when(has_left)
        def _():
            sum_copy(0, z, k, right).wait_recv()

        @pl.when(has_right)
        def _():
            sum_copy(1, z, k, left).wait_recv()

        own = part[z, k].astype(F32)
        own += jnp.where(has_left, rbuf[0, z, k].astype(F32), 0.0)
        own += jnp.where(has_right, rbuf[1, z, k].astype(F32), 0.0)
        fin[k] = own.astype(BF16).reshape(two, CAP, span)
        result_copy(c, k).start()
        ret[c, k] = fin[k, c]

    cw = jnp.transpose(jnp.concatenate(combine, axis=0))
    first = cw.astype(BF16)
    rest = cw - first.astype(F32)
    second = rest.astype(BF16)
    third = (rest - second.astype(F32)).astype(BF16)
    for k in range(KV_HEADS):
        cols = slice(k * span, (k + 1) * span)
        result_copy(sib, k).wait_recv()
        returned = ret[:, k].reshape(rows_here, span)
        total = (
            jnp.dot(first, returned, preferred_element_type=F32)
            + jnp.dot(second, returned, preferred_element_type=F32)
            + jnp.dot(third, returned, preferred_element_type=F32)
        )
        out_ref[:, cols] = (att[k].astype(F32) + total).astype(BF16)

    def drain(h, carry):
        result_copy(c, h).wait_send()
        sib_copy(h).wait_send()
        if ship:
            @pl.when(is_end & (h < ship))
            def _():
                query_copy(h).wait_send()

            @pl.when(helps & (h < ship))
            def _():
                answer_copy(h).wait_send()

        for oz in range(n):
            @pl.when(goes_left(h) & (oz >= z))
            def _():
                kv_copy(h, oz, c, 0, left).wait_send()

            @pl.when(goes_right(h) & (oz <= z))
            def _():
                kv_copy(h, oz, c, 1, right).wait_send()

            @pl.when(gathers(h))
            def _():
                kv_copy(h, oz, c, 2, other).wait_send()

            @pl.when(has_left & (oz >= z))
            def _():
                row_copy(oz, h, 0, left).wait_send()

            @pl.when(has_right & (oz <= z))
            def _():
                row_copy(oz, h, 1, right).wait_send()

            @pl.when(oz > z)
            def _():
                sum_copy(0, oz, h, right).wait_send()

            @pl.when(oz < z)
            def _():
                sum_copy(1, oz, h, left).wait_send()
        return carry

    lax.fori_loop(0, KV_HEADS, drain, 0)


def body(
    queries, keys_values, prompt_lengths, routes, gate_weights, norm_gain, w_gate, w_up, w_down
):
    n = lax.axis_size("seq")
    tokens, width = queries.shape[1:]
    piece = keys_values.shape[1]
    ff = w_gate.shape[2]
    span = width // KV_HEADS
    top = routes.shape[2]
    vmem = pl.BlockSpec(memory_space=pltpu.VMEM)
    hbm = pl.BlockSpec(memory_space=pltpu.HBM)
    dma = pltpu.SemaphoreType.DMA
    mixed = pl.pallas_call(
        functools.partial(kernel, n),
        out_shape=jax.ShapeDtypeStruct((tokens, width), BF16),
        in_specs=[pl.BlockSpec(memory_space=pltpu.SMEM)] + [hbm] * 8,
        out_specs=vmem,
        scratch_shapes=[
            pltpu.VMEM((top, tokens), jnp.int32),
            pltpu.VMEM((top, tokens), F32),
            pltpu.VMEM((1, width), F32),
            pltpu.VMEM((KV_HEADS, piece, 2, HEAD_DIM), BF16),
            pltpu.VMEM((KV_HEADS, tokens, span), BF16),
            pltpu.VMEM((KV_HEADS, tokens, span), BF16),
            pltpu.VMEM((KV_HEADS, tokens, span), BF16),
            pltpu.VMEM((width, ff), BF16),
            pltpu.VMEM((width, ff), BF16),
            pltpu.VMEM((ff, width), BF16),
            pltpu.VMEM((KV_HEADS, 2, n, 2, piece, HEAD_DIM), BF16),
            pltpu.VMEM((KV_HEADS, tokens, span), BF16),
            pltpu.VMEM((2 * CAP, tokens), BF16),
            pltpu.VMEM((KV_HEADS, 2, CAP, span), BF16),
            pltpu.VMEM((n, KV_HEADS, 2, CAP, span), BF16),
            pltpu.VMEM((n, KV_HEADS, 2 * CAP, span), BF16),
            pltpu.VMEM((2, n, KV_HEADS, 2 * CAP, span), BF16),
            pltpu.VMEM((KV_HEADS, 2, CAP, span), BF16),
            pltpu.VMEM((2, KV_HEADS, CAP, span), BF16),
            dma((3,)),
            dma((3,)),
            dma((KV_HEADS,)),
            dma((KV_HEADS,)),
            dma((KV_HEADS, n, 3)),
            dma((KV_HEADS, n, 2)),
            dma((KV_HEADS,)),
            dma((KV_HEADS,)),
            dma((KV_HEADS,)),
            dma((KV_HEADS,)),
            dma((KV_HEADS,)),
            dma((KV_HEADS,)),
            dma((n, KV_HEADS, 2)),
            dma((n, KV_HEADS)),
            dma((2, n, KV_HEADS)),
            dma((2, n, KV_HEADS)),
            dma((KV_HEADS,)),
            dma((KV_HEADS,)),
        ],
        compiler_params=pltpu.CompilerParams(
            collective_id=0, has_side_effects=True, vmem_limit_bytes=48 * 1024 * 1024
        ),
    )(
        prompt_lengths,
        *[
            pltpu.with_memory_space_constraint(operand, pltpu.HBM)
            for operand in (
                routes[0].T, gate_weights[0].T, norm_gain[None], keys_values[0], queries[0],
                w_gate[0], w_up[0], w_down[0],
            )
        ],
    )
    return mixed[None]


def solution(mesh):
    return jax.shard_map(
        body,
        mesh=mesh,
        in_specs=(
            P(("group", "exp"), ("seq", "tp"), None),
            P(("group", "exp"), ("seq", "tp"), None, None),
            P(("group", "exp")),
            P(("group", "exp"), ("seq", "tp"), None),
            P(("group", "exp"), ("seq", "tp"), None),
            P(),
            P("tp", None, "seq"),
            P("tp", None, "seq"),
            P("tp", "seq", None),
        ),
        out_specs=P(("group", "exp"), ("seq", "tp"), None),
        check_vma=False,
    )
```

time: 79.3 us -> 75.3 us (0.950)
  local copies, waits for them, and re-layouts: 3.69 us -> 0.8 us
  Pallas kernels: 74.8 us -> 73.7 us
    unnamed x2 -> x1, local copies, waits for them, and re-layouts: 3.69 us -> 0.8 us
    pallas_call x1, Pallas kernels: 74.8 us -> 73.7 us  [body(): pl.pallas_call(functools.partial(kernel, n), out_shape=jax.ShapeDtypeStru...]
where the time goes in v1:
time: 75.3 us; the launch traced here: 75.1 us
  Pallas kernels  73.7 us (98%)
  local copies, waits for them, and re-layouts  0.8 us (1%)
    pallas_call x1, Pallas kernels, body(): pl.pallas_call(functools.partial(kernel, n), out_shape=jax.ShapeDtypeStru...  73.7 us

profile of v1, /device:TPU:0, one launch (start us, length us, event | category | flops | bytes accessed | tf_op | source)
XLA Modules:
  0.0 75.1 jit_solution(13664965331340055431)
XLA Ops:
  0.7 73.7 %shard_map.91 = bf16[64,4096]{1,0:T(8,128)(2,1)S(1)} custom-call(s32[1]{0:T(128)S(6)} %copy.11.plen_ref, s32[8,64]{1,0:T(8,128)} %bitcast.20, f32[8,64]{1,0:T(8,128)} %bitcast.21, f32[1,4096]{1,0:T(1,128)} %bitcast.19, bf16[96,2,1024]{2,1,0:T(2,128)(2,1)} %bitcast.18, bf16[64,4096]{1,0:T(8,128)(2,1)} %bitcast.17, bf16[4096,512]{1,0:T(8,128)(2,1)} %bitcast.14, ...), custom_call_target="tpu_custom_call" | custom-call | tf_op jit(solution)/shard_map/pallas_call | solution.py:500
  74.4 0.8 %copy.12 = bf16[1,64,4096]{2,1,0:T(8,128)(2,1)} copy(bf16[1,64,4096]{2,1,0:T(8,128)(2,1)S(1)} %bitcast.13) | data formatting | bytes 1048576
